TPU v7x, 256 devices: a whole 4x4x8 slice. The times are simulated.
256 devices in a mesh: gx: 16 (over y_lo, x, core), ch: 16 (over z, y_hi).
Axes of the slice: x: 4, y: 4 (y_hi: 2, y_lo: 2; y = y_hi * 2 + y_lo), z: 8, core: 2. Of those that a mesh axis runs over, the one named last changes fastest.
Arguments:
- activations: bfloat16 [128, 256, 4, 128], P('ch', 'gx'), may hold values from -6 to 6
- conv_weight: bfloat16 [27, 128, 128], P(None, None, 'ch'), may hold values from -0.109375 to 0.109375
- out_grad: bfloat16 [128, 256, 4, 128], P('ch', 'gx'), may hold values from -6 to 6
Outputs:
- features_out: bfloat16 [128, 256, 4, 128], P('ch', 'gx')
- input_grad: bfloat16 [128, 256, 4, 128], P('ch', 'gx')
All inputs are finite; a program needn't handle non-finite values.
Results may differ from a plain program's by a relative error of at most 0.001.
Values may be sent and summed in bfloat16 or wider, within the bound.
No kernel may reach another device: no remote copies, remote signals or barrier semaphores. Data moves between devices by JAX's collectives and lax.ppermute only.
A program may use at most 64 MiB of HBM per device.

v0:
```python
import jax
import jax.numpy as jnp
from jax import lax
from jax.sharding import PartitionSpec as P


def with_halo(cells, sides, width):
    for axis, dim in sides:
        count = lax.axis_size(axis)
        head = lax.slice_in_dim(cells, 0, width, axis=dim)
        tail = lax.slice_in_dim(cells, cells.shape[dim] - width, cells.shape[dim], axis=dim)
        cells = jnp.concatenate(
            [
                lax.ppermute(tail, axis, [(i, (i + 1) % count) for i in range(count)]),
                cells,
                lax.ppermute(head, axis, [((i + 1) % count, i) for i in range(count)]),
            ],
            axis=dim,
        )
    return cells


def tap_sum(extended, weight, direction, pattern):
    planes = extended.shape[1] - 2
    depth = extended.shape[2]
    height = extended.shape[3]
    padded = jnp.pad(extended, ((0, 0), (0, 0), (1, 1), (1, 1)))
    summed = None
    for first in range(3):
        for second in range(3):
            for third in range(3):
                offset_x = 1 + direction * (first - 1)
                offset_y = 1 + direction * (second - 1)
                offset_z = 1 + direction * (third - 1)
                window_part = padded[
                    :,
                    offset_x : offset_x + planes,
                    offset_z : offset_z + depth,
                    offset_y : offset_y + height,
                ]
                product = jnp.einsum(
                    pattern,
                    window_part,
                    weight[9 * first + 3 * second + third],
                    preferred_element_type=jnp.float32,
                )
                summed = product if summed is None else summed + product
    return summed


def slab_faces(field):
    return with_halo(field, (("gx", 1),), 1)


def local(activations, conv_weight, out_grad):
    full_weight = lax.all_gather(conv_weight, "ch", axis=2, tiled=True)
    local_rows = activations.shape[0]
    extended_act = slab_faces(activations)
    sliced = conv_weight
    features_out = tap_sum(
        lax.all_gather(extended_act, "ch", axis=0, tiled=True), sliced, 1, "kxzy,kn->nxzy"
    ).astype(jnp.bfloat16)
    extended_grad = slab_faces(out_grad)
    own_start = lax.axis_index("ch") * local_rows
    weight_rows = lax.dynamic_slice_in_dim(full_weight, own_start, local_rows, 1)
    sliced = weight_rows
    input_grad = tap_sum(
        lax.all_gather(extended_grad, "ch", axis=0, tiled=True), sliced, -1, "kxzy,nk->nxzy"
    ).astype(jnp.bfloat16)
    return (features_out, input_grad)


def solution(mesh):
    return jax.shard_map(
        local,
        mesh=mesh,
        in_specs=(P("ch", "gx", None, None), P(None, None, "ch"), P("ch", "gx", None, None)),
        out_specs=(P("ch", "gx", None, None), P("ch", "gx", None, None)),
        check_vma=False,
    )
```

profile of v0, /device:TPU:2, one launch (start us, length us, event | category | flops | bytes accessed | tf_op | source)
XLA Modules:
  0.0 219.0 jit_solution(10602987286998030668)
XLA Ops:
  7.2 1.0 copy.18
  8.3 1.7 collective-permute-start.3
  10.0 1.3 collective-permute-done.2
  11.4 0.7 pad_maximum_fusion.1
  12.2 1.0 copy.14
  13.2 1.6 collective-permute-start
  15.0 1.3 collective-permute-done
  16.4 0.7 pad_maximum_fusion
  17.1 53.9 %all_gather.10 = bf16[27,128,128]{1,2,0:T(8,128)(2,1)S(1)} all-gather(bf16[27,128,8]{1,2,0:T(8,128)(2,1)} %param.4), channel_id=1, replica_groups=mesh['gx'=16,'ch'=16] {'ch'}, dimensions={2}, use_global_device_ids=true | all-gather | bytes 940032 | tf_op jit(solution)/shard_map/all_gather | solution.py:56
  71.0 36.9 %all-gather.5.cloned.1.call-done = bf16[128,18,4,128]{3,0,2,1:T(8,128)(2,1)} async-done(((bf16[8,18,4,128]{3,0,2,1:T(8,128)(2,1)}), bf16[128,18,4,128]{3,0,2,1:T(8,128)(2,1)}) %all-gather.5.cloned.1.call-update) | async-done | bytes 2359312 | tf_op jit(solution)/shard_map/all_gather | solution.py:68
  107.9 2.1 fusion.10
  110.7 0.8 fusion.12
  112.7 0.8 fusion.15
  115.2 0.7 fusion.19
  115.8 0.8 fusion.20
  117.9 0.8 fusion.23
  120.4 0.7 fusion.27
  121.0 0.8 fusion.28
  122.5 0.8 fusion.7
  124.4 0.7 fusion
  126.2 0.8 fusion.116
  127.0 0.7 copy.22
  127.7 66.4 %all-gather.3.cloned.1.call-done = bf16[128,18,4,128]{3,0,2,1:T(8,128)(2,1)} async-done(((bf16[8,18,4,128]{3,0,2,1:T(8,128)(2,1)}), bf16[128,18,4,128]{3,0,2,1:T(8,128)(2,1)}) %all-gather.3.cloned.1.call-update) | async-done | bytes 2359312 | tf_op jit(solution)/shard_map/all_gather | solution.py:61
  194.2 2.1 fusion.158
  196.8 0.7 fusion.31
  199.5 0.7 fusion.36
  201.4 0.7 fusion.39
  204.1 0.7 fusion.44
  206.2 0.7 fusion.60
  208.1 1.0 fusion.55
  209.7 0.7 fusion.107
  211.4 0.7 copy.21
  (51 shorter events, 19.9 us)
Async XLA Ops:
  7.2 100.7 %all-gather.5.cloned.1.call-start = ((), (), s32[]{:S(2)}) async-start(), calls=%async_computation.1 | async-start | bytes 2506752 | tf_op jit(solution)/shard_map/all_gather | solution.py:68
  8.2 3.2 %collective-permute-start.2 = (bf16[8,1,4,128]{3,0,2,1:T(8,128)(2,1)S(1)}, bf16[8,1,4,128]{3,0,2,1:T(8,128)(2,1)S(1)}, u32[]{:S(2)}, u32[]{:S(2)}) collective-permute-start(bf16[8,1,4,128]{3,0,2,1:T(8,128)(2,1)S(1)} %get-tuple-element.6), channel_id=1, source_target_pairs={{0,16},{16,32},{32,48},{48,64},{64,80},{80,96},{96,112},{112,128},... | collective-permute-start | bytes 24584 | tf_op jit(solution)/shard_map/ppermute | solution.py:14
  8.3 3.1 %collective-permute-start.3 = (bf16[8,1,4,128]{3,0,2,1:T(8,128)(2,1)S(1)}, bf16[8,1,4,128]{3,0,2,1:T(8,128)(2,1)S(1)}, u32[]{:S(2)}, u32[]{:S(2)}) collective-permute-start(bf16[8,1,4,128]{3,0,2,1:T(8,128)(2,1)S(1)} %get-tuple-element.7), channel_id=1, source_target_pairs={{16,0},{32,16},{48,32},{64,48},{80,64},{96,80},{112,96},{128,112},... | collective-permute-start | bytes 24584 | tf_op jit(solution)/shard_map/ppermute | solution.py:16
  12.1 182.1 %all-gather.3.cloned.1.call-start = ((), (), s32[]{:S(2)}) async-start(), calls=%async_computation | async-start | bytes 2506752 | tf_op jit(solution)/shard_map/all_gather | solution.py:61
  13.2 3.2 %collective-permute-start = (bf16[8,1,4,128]{3,0,2,1:T(8,128)(2,1)S(1)}, bf16[8,1,4,128]{3,0,2,1:T(8,128)(2,1)S(1)}, u32[]{:S(2)}, u32[]{:S(2)}) collective-permute-start(bf16[8,1,4,128]{3,0,2,1:T(8,128)(2,1)S(1)} %get-tuple-element.8), channel_id=1, source_target_pairs={{0,16},{16,32},{32,48},{48,64},{64,80},{80,96},{96,112},{112,128},... | collective-permute-start | bytes 24584 | tf_op jit(solution)/shard_map/ppermute | solution.py:14
  14.8 1.6 collective-permute-start.1
  107.9 2.1 copy-start.1
  126.2 68.0 %copy-start.2 = (bf16[27,128,8]{1,2,0:T(8,128)(2,1)S(1)}, bf16[27,128,8]{1,2,0:T(8,128)(2,1)}, u32[]{:S(2)}) copy-start(bf16[27,128,8]{1,2,0:T(8,128)(2,1)} %param.4) | copy-start | bytes 165892
  194.2 2.3 %copy-start = (bf16[128,18,4,128]{3,0,2,1:T(8,128)(2,1)S(1)}, bf16[128,18,4,128]{3,0,2,1:T(8,128)(2,1)}, u32[]{:S(2)}) copy-start(bf16[128,18,4,128]{3,0,2,1:T(8,128)(2,1)} %all-gather.3.cloned.1.call-done) | copy-start | bytes 7077892
Sparse Core Ops, SparseCore 0:
  12.2 95.5 all-gather.4
  110.3 83.7 all-gather.2
where the time goes:
time: 219 us
  waiting for transfers between devices  106 us (48%)
  blocking collectives  53.9 us (25%)
  matrix products  36.1 us (16%)
  between operations  14.1 us (6%)
  starting transfers between devices  3.77 us (2%)
  local copies, waits for them, and re-layouts  3.68 us (2%)
    all_gather x1, waiting for transfers between devices, local(): lax.all_gather(extended_act, 'ch', axis=0, tiled=True)  66.4 us
    all_gather x1, blocking collectives, local(): full_weight = lax.all_gather(conv_weight, 'ch', axis=2, tiled=True)  53.9 us
    all_gather x1, waiting for transfers between devices, local(): lax.all_gather(extended_grad, 'ch', axis=0, tiled=True)  36.9 us
    dot_general x54, matrix products, tap_sum(): jnp.einsum(pattern, window_part, weight[9 * first + 3 * second + third],...  36.1 us
  transfers between devices with their start and end apart: 6, of which 5 were waited for; matrix products, arithmetic and copies ran while one was open for 10% of the time, Pallas kernels for 0%

commit v1 on v0

--- a/solution.py
+++ b/solution.py
@@ -58,7 +58,12 @@
     extended_act = slab_faces(activations)
     sliced = conv_weight
     features_out = tap_sum(
-        lax.all_gather(extended_act, "ch", axis=0, tiled=True), sliced, 1, "kxzy,kn->nxzy"
+        jnp.concatenate(
+            lax.all_to_all(jnp.stack([extended_act] * lax.axis_size("ch")), "ch", 0, 0), axis=0
+        ),
+        sliced,
+        1,
+        "kxzy,kn->nxzy",
     ).astype(jnp.bfloat16)
     extended_grad = slab_faces(out_grad)
     own_start = lax.axis_index("ch") * local_rows

time: 219 us -> 192 us (0.88)
  waiting for transfers between devices: 106 us -> 16.6 us
  blocking collectives: 53.9 us -> 103 us
  starting transfers between devices: 3.77 us -> 15.3 us
    all_gather x1 -> x0, waiting for transfers between devices: 66.4 us -> none  [local(): lax.all_gather(extended_act, 'ch', axis=0, tiled=True)]
    all_gather x1, blocking collectives: 53.9 us -> 103 us  [local(): full_weight = lax.all_gather(conv_weight, 'ch', axis=2, tiled=True)]
    all_gather x1, waiting for transfers between devices: 36.9 us -> 13.9 us  [local(): lax.all_gather(extended_grad, 'ch', axis=0, tiled=True)]
    all_to_all x0 -> x1, starting transfers between devices: none -> 11.6 us  [local(): lax.all_to_all(jnp.stack([extended_act] * lax.axis_size('ch')), 'ch', 0, 0)]
  transfers between devices with their start and end apart: 6 -> 6, of which waited for: 5 -> 4; matrix products, arithmetic and copies ran while one was open for 10% -> 12% of each run, Pallas kernels for 0% -> 0%
where the time goes in v1:
time: 192 us; the launch traced here: 191 us
  blocking collectives  103 us (54%)
  matrix products  34.3 us (18%)
  waiting for transfers between devices  16.6 us (9%)
  starting transfers between devices  15.3 us (8%)
  between operations  14.1 us (7%)
  local copies, waits for them, and re-layouts  5.78 us (3%)
    all_gather x1, blocking collectives, local(): full_weight = lax.all_gather(conv_weight, 'ch', axis=2, tiled=True)  103 us
    dot_general x54, matrix products, tap_sum(): jnp.einsum(pattern, window_part, weight[9 * first + 3 * second + third],...  34.3 us
    all_gather x1, waiting for transfers between devices, local(): lax.all_gather(extended_grad, 'ch', axis=0, tiled=True)  13.9 us
    all_to_all x1, starting transfers between devices, local(): lax.all_to_all(jnp.stack([extended_act] * lax.axis_size('ch')), 'ch', 0, 0)  11.6 us
  transfers between devices with their start and end apart: 6, of which 4 were waited for; matrix products, arithmetic and copies ran while one was open for 12% of the time, Pallas kernels for 0%

profile of v1, /device:TPU:2, one launch (start us, length us, event | category | flops | bytes accessed | tf_op | source)
XLA Modules:
  0.0 190.5 jit_solution(2713305891705698201)
XLA Ops:
  7.2 1.0 copy.15
  8.3 1.7 collective-permute-start.3
  10.0 1.3 collective-permute-done.2
  11.4 0.7 pad_maximum_fusion.1
  12.1 0.7 fusion.250
  12.8 1.6 collective-permute-start
  14.7 1.3 collective-permute-done
  16.1 1.0 pad_maximum_fusion
  17.1 1.9 stack.2
  19.0 11.6 %all-to-all-start = ((bf16[16,8,18,4,128]{4,1,3,2,0:T(8,128)(2,1)}), bf16[16,8,18,4,128]{4,1,3,2,0:T(8,128)(2,1)S(1)}, u32[]{:S(2)}, u32[]{:S(2)}) async-start(bf16[16,8,18,4,128]{4,1,3,2,0:T(8,128)(2,1)} %stack.2), calls=%async_computation | async-start | bytes 4718592 | tf_op jit(solution)/shard_map/all_to_all | solution.py:62
  30.6 102.6 %all_gather.6 = bf16[27,128,128]{1,2,0:T(8,128)(2,1)S(1)} all-gather(bf16[27,128,8]{1,2,0:T(8,128)(2,1)S(1)} %copy-done.1), channel_id=1, replica_groups=mesh['gx'=16,'ch'=16] {'ch'}, dimensions={2}, use_global_device_ids=true | all-gather | bytes 940032 | tf_op jit(solution)/shard_map/all_gather | solution.py:56
  133.3 13.9 %all-gather.2.cloned.1.call-done = bf16[128,18,4,128]{3,0,2,1:T(8,128)(2,1)} async-done(((bf16[8,18,4,128]{3,0,2,1:T(8,128)(2,1)}), bf16[128,18,4,128]{3,0,2,1:T(8,128)(2,1)}) %all-gather.2.cloned.1.call-update) | async-done | bytes 2359312 | tf_op jit(solution)/shard_map/all_gather | solution.py:73
  147.1 2.1 %fusion.10 = f32[8,16,4,128]{3,0,2,1:T(8,128)S(1)} fusion(bf16[128,18,4,128]{3,0,2,1:T(8,128)(2,1)} %all-gather.2.cloned.1.call-done, bf16[27,128,128]{1,2,0:T(8,128)(2,1)S(1)} %all_gather.6, s32[]{:T(128)S(6)} %add.239, s32[]{:T(128)S(6)} %select_n.3), kind=kOutput, calls=%fused_computation.59 | convolution fusion | flops 16777216 | bytes 2654216 | tf_op jit(solution)/shard_map/kxzy,nk->nxzy/dot_general | solution.py:41
  149.9 0.8 fusion.12
  152.0 0.8 fusion.15
  154.5 0.7 fusion.19
  155.1 0.8 fusion.20
  157.2 0.8 fusion.23
  160.3 0.8 fusion.28
  161.7 0.8 fusion.7
  163.7 0.7 fusion
  165.4 0.8 fusion.116
  166.3 0.7 copy.19
  167.0 0.7 copy.106
  168.3 0.7 fusion.86
  171.4 0.7 fusion.81
  173.3 0.7 fusion.78
  176.4 0.7 fusion.73
  178.3 0.7 fusion.65
  179.0 0.9 fusion.66
  181.7 0.7 fusion.70
  183.0 0.7 copy.18
  (50 shorter events, 20.7 us)
Async XLA Ops:
  7.2 140.0 %all-gather.2.cloned.1.call-start = ((), (), s32[]{:S(2)}) async-start(), calls=%async_computation.1 | async-start | bytes 2506752 | tf_op jit(solution)/shard_map/all_gather | solution.py:73
  8.2 3.2 %collective-permute-start.2 = (bf16[8,1,4,128]{3,0,2,1:T(8,128)(2,1)S(1)}, bf16[8,1,4,128]{3,0,2,1:T(8,128)(2,1)S(1)}, u32[]{:S(2)}, u32[]{:S(2)}) collective-permute-start(bf16[8,1,4,128]{3,0,2,1:T(8,128)(2,1)S(1)} %get-tuple-element.6), channel_id=1, source_target_pairs={{0,16},{16,32},{32,48},{48,64},{64,80},{80,96},{96,112},{112,128},... | collective-permute-start | bytes 24584 | tf_op jit(solution)/shard_map/ppermute | solution.py:14
  8.3 3.1 %collective-permute-start.3 = (bf16[8,1,4,128]{3,0,2,1:T(8,128)(2,1)S(1)}, bf16[8,1,4,128]{3,0,2,1:T(8,128)(2,1)S(1)}, u32[]{:S(2)}, u32[]{:S(2)}) collective-permute-start(bf16[8,1,4,128]{3,0,2,1:T(8,128)(2,1)S(1)} %get-tuple-element.7), channel_id=1, source_target_pairs={{16,0},{32,16},{48,32},{64,48},{80,64},{96,80},{112,96},{128,112},... | collective-permute-start | bytes 24584 | tf_op jit(solution)/shard_map/ppermute | solution.py:16
  12.8 3.1 %collective-permute-start = (bf16[8,1,4,128]{3,2,1,0:T(4,128)(2,1)S(1)}, bf16[8,1,4,128]{3,2,1,0:T(4,128)(2,1)S(1)}, u32[]{:S(2)}, u32[]{:S(2)}) collective-permute-start(bf16[8,1,4,128]{3,2,1,0:T(4,128)(2,1)S(1)} %get-tuple-element.8), channel_id=1, source_target_pairs={{0,16},{16,32},{32,48},{48,64},{64,80},{80,96},{96,112},{112,128},... | collective-permute-start | bytes 24584 | tf_op jit(solution)/shard_map/ppermute | solution.py:14
  14.5 1.6 collective-permute-start.1
  19.0 11.6 %copy-start.1 = (bf16[27,128,8]{1,2,0:T(8,128)(2,1)S(1)}, bf16[27,128,8]{1,2,0:T(8,128)(2,1)}, u32[]{:S(2)}) copy-start(bf16[27,128,8]{1,2,0:T(8,128)(2,1)} %param.4) | copy-start | bytes 165892
  19.0 148.0 %all-to-all-start = ((bf16[16,8,18,4,128]{4,1,3,2,0:T(8,128)(2,1)}), bf16[16,8,18,4,128]{4,1,3,2,0:T(8,128)(2,1)S(1)}, u32[]{:S(2)}, u32[]{:S(2)}) async-start(bf16[16,8,18,4,128]{4,1,3,2,0:T(8,128)(2,1)} %stack.2), calls=%async_computation | async-start | bytes 4718592 | tf_op jit(solution)/shard_map/all_to_all | solution.py:62
  147.1 2.1 %copy-start = (bf16[128,18,4,128]{3,0,2,1:T(8,128)(2,1)S(1)}, bf16[128,18,4,128]{3,0,2,1:T(8,128)(2,1)}, u32[]{:S(2)}) copy-start(bf16[128,18,4,128]{3,0,2,1:T(8,128)(2,1)} %all-gather.2.cloned.1.call-done) | copy-start | bytes 7077892
Sparse Core Ops, SparseCore 0:
  12.2 134.8 all-gather.1
